TPU v7x, 32 devices: a whole 2x2x4 slice. The times are simulated.
32 devices in a mesh: grp: 2 (over y), gx: 4 (over z), gy: 4 (over x, core).
Axes of the slice: x: 2, y: 2, z: 4, core: 2. Of those that a mesh axis runs over, the one named last changes fastest.
Arguments:
- input_activation: bfloat16 [32, 32, 1024], P(('grp', 'gx'), 'gy'), parts along dimension 0, may hold values from -6 to 6
- pre_one: bfloat16 [32, 32, 1024], P(('grp', 'gx'), 'gy'), parts along dimension 0, may hold values from -6 to 6
- pre_two: bfloat16 [32, 32, 1024], P(('grp', 'gx'), 'gy'), parts along dimension 0, may hold values from -6 to 6
- w_one: bfloat16 [27, 64, 64], replicated, may hold values from -0.15625 to 0.15625
- w_two: bfloat16 [27, 64, 64], replicated, may hold values from -0.15625 to 0.15625
- w_trans: bfloat16 [512, 512], replicated, may hold values from -0.5 to 0.5
- keep_mask: int32 [8, 8], replicated, may hold values 0 or 1
- out_grad: bfloat16 [16, 16, 8, 512], P('grp', 'gy', None, 'gx'), parts along dimension 0, may hold values from -6 to 6
Outputs:
- grad_in: bfloat16 [32, 32, 1024], P(('grp', 'gx'), 'gy'), parts along dimension 0
- grad_w_one: float32 [54, 64, 64], P('grp'), parts along dimension 0
- grad_w_two: float32 [54, 64, 64], P('grp'), parts along dimension 0
- grad_w_trans: float32 [1024, 512], P('grp'), parts along dimension 0
There are 2 independent parts, one for each index of `grp`. A program takes and returns all parts, laid end to end along the dimension named above; an argument that names none is the same for every part. Nothing has to cross between parts.
All inputs are finite; a program needn't handle non-finite values.
Results may differ from a plain program's by a relative error of at most 0.0058.
Values may be sent and summed in bfloat16 or wider, within the bound.
No kernel may reach another device: no remote copies, remote signals or barrier semaphores. Data moves between devices by JAX's collectives and lax.ppermute only.
A program may use at most 64 MiB of HBM per device.

v0:
```python
import math
import jax
import jax.numpy as jnp
from jax import lax
from jax.sharding import PartitionSpec as P

DILATION_STEP = 2


def padded(cells, sides, width):
    for axis, dim in sides:
        count = lax.axis_size(axis)
        ends = count - 1
        head = lax.slice_in_dim(cells, 0, width, axis=dim)
        tail = lax.slice_in_dim(cells, cells.shape[dim] - width, cells.shape[dim], axis=dim)
        cells = jnp.concatenate(
            [
                lax.ppermute(tail, axis, [(i, (i + 1) % count) for i in range(ends)]),
                cells,
                lax.ppermute(head, axis, [((i + 1) % count, i) for i in range(ends)]),
            ],
            axis=dim,
        )
    return cells


def split_layout(joined_layout, channel_count):
    return joined_layout.reshape(joined_layout.shape[0], joined_layout.shape[1], -1, channel_count)


def to_blocks(cube_volume):
    shape_all = cube_volume.shape
    parted = cube_volume.reshape(
        shape_all[0] // 2, 2, shape_all[1] // 2, 2, shape_all[2] // 2, 2, shape_all[3]
    )
    parted = parted.transpose(0, 2, 4, 1, 3, 5, 6)
    return parted.reshape(shape_all[0] // 2, shape_all[1] // 2, shape_all[2] // 2, 8 * shape_all[3])


def from_blocks(blocked, channel_count):
    shape_all = blocked.shape
    parted = blocked.reshape(shape_all[0], shape_all[1], shape_all[2], 2, 2, 2, channel_count)
    parted = parted.transpose(0, 3, 1, 4, 2, 5, 6)
    return parted.reshape(2 * shape_all[0], 2 * shape_all[1], 2 * shape_all[2], channel_count)


def padding_depth(cube_volume, margin):
    return jnp.pad(cube_volume, ((0, 0), (0, 0), (margin, margin), (0, 0)))


def weight_terms(bordered_input, upstream_gradient):
    channel_count = upstream_gradient.shape[3]
    grid_extent = upstream_gradient.shape
    padded_input = padding_depth(bordered_input, DILATION_STEP)
    flat_grad = upstream_gradient.reshape(-1, channel_count)
    partials = []
    for x_index in range(3):
        for y_index in range(3):
            sliding_window = padded_input[
                DILATION_STEP * x_index : DILATION_STEP * x_index + grid_extent[0],
                DILATION_STEP * y_index : DILATION_STEP * y_index + grid_extent[1],
            ]
            columns = jnp.concatenate(
                [
                    sliding_window[
                        :, :, DILATION_STEP * tap_index : DILATION_STEP * tap_index + grid_extent[2]
                    ].reshape(-1, channel_count)
                    for tap_index in range(3)
                ],
                axis=1,
            )
            partials.append(
                lax.dot_general(
                    columns, flat_grad, (((0,), (0,)), ((), ())), preferred_element_type=jnp.float32
                )
            )
    return jnp.stack(partials).reshape(27, channel_count, channel_count)


def data_terms(bordered_input, weights):
    channel_count = weights.shape[1]
    x_stretch = bordered_input.shape[0] - 2 * DILATION_STEP
    y_stretch = bordered_input.shape[1] - 2 * DILATION_STEP
    depth_cells = bordered_input.shape[2]
    padded_input = padding_depth(bordered_input, DILATION_STEP)
    stacked = jnp.transpose(weights, (0, 2, 1)).reshape(9, 3 * channel_count, channel_count)
    running = jnp.zeros((x_stretch * y_stretch * depth_cells, channel_count), jnp.float32)
    for x_index in range(3):
        for y_index in range(3):
            sliding_window = padded_input[
                DILATION_STEP * (2 - x_index) : DILATION_STEP * (2 - x_index) + x_stretch,
                DILATION_STEP * (2 - y_index) : DILATION_STEP * (2 - y_index) + y_stretch,
            ]
            columns = jnp.concatenate(
                [
                    sliding_window[
                        :,
                        :,
                        DILATION_STEP * (2 - tap_index) : DILATION_STEP * (2 - tap_index)
                        + depth_cells,
                    ].reshape(-1, channel_count)
                    for tap_index in range(3)
                ],
                axis=1,
            )
            running = running + jnp.dot(
                columns, stacked[x_index * 3 + y_index], preferred_element_type=jnp.float32
            )
    return running.reshape(x_stretch, y_stretch, depth_cells, channel_count)


def body(input_activation, pre_one, pre_two, w_one, w_two, w_trans, keep_mask, out_grad):
    channel_count = w_one.shape[1]
    x_stretch, y_stretch, joined_layout = input_activation.shape
    depth_cells = joined_layout // channel_count
    width_t = w_trans.shape[0]
    factor = 1.0 / math.sqrt(
        x_stretch * lax.axis_size("gx") * y_stretch * lax.axis_size("gy") * depth_cells
    )
    blocks = jnp.repeat(
        jnp.repeat(keep_mask.astype(jnp.bfloat16), channel_count, axis=0), channel_count, axis=1
    )
    w_kept = w_trans * blocks
    regrouped = lax.all_to_all(out_grad, "gx", split_axis=0, concat_axis=3, tiled=True)
    grad_rows = regrouped.reshape(-1, width_t)
    back_blocks = lax.dot_general(
        grad_rows, w_kept, (((1,), (1,)), ((), ())), preferred_element_type=jnp.float32
    ).astype(jnp.bfloat16)
    act_two = split_layout(jnp.maximum(pre_two, 0), channel_count)
    two_rows = to_blocks(act_two).reshape(-1, width_t)
    trans_term = (
        lax.dot_general(
            two_rows, grad_rows, (((0,), (0,)), ((), ())), preferred_element_type=jnp.float32
        )
        * blocks.astype(jnp.float32)
        * factor
    )
    grad_w_trans = lax.psum(trans_term, ("gx", "gy"))
    back_two = from_blocks(
        back_blocks.reshape(x_stretch // 2, y_stretch // 2, depth_cells // 2, width_t),
        channel_count,
    )
    back_two = jnp.where(
        split_layout(pre_two, channel_count) > 0, back_two, jnp.zeros_like(back_two)
    )
    first_activation = jnp.maximum(pre_one, 0)
    bordered_input = padded(
        jnp.concatenate([input_activation, first_activation], axis=2),
        (("gx", 0), ("gy", 1)),
        DILATION_STEP,
    )
    in_rim = split_layout(bordered_input[:, :, :joined_layout], channel_count)
    one_rim = split_layout(bordered_input[:, :, joined_layout:], channel_count)
    two_term = weight_terms(one_rim, back_two) * factor
    flattened_backward = back_two.reshape(x_stretch, y_stretch, joined_layout)
    narrowed_slice = split_layout(
        padded(flattened_backward, (("gx", 0), ("gy", 1)), DILATION_STEP), channel_count
    )
    first_backward = data_terms(narrowed_slice, w_two)
    first_backward = jnp.where(
        split_layout(pre_one, channel_count) > 0, first_backward, jnp.zeros_like(first_backward)
    ).astype(jnp.bfloat16)
    one_grad_rim = split_layout(
        padded(
            first_backward.reshape(x_stretch, y_stretch, joined_layout),
            (("gx", 0), ("gy", 1)),
            DILATION_STEP,
        ),
        channel_count,
    )
    grad_w_two = lax.psum(two_term, ("gx", "gy"))
    one_term = weight_terms(in_rim, first_backward) * factor
    grad_w_one = lax.psum(one_term, ("gx", "gy"))
    grad_in = (
        data_terms(one_grad_rim, w_one)
        .astype(jnp.bfloat16)
        .reshape(x_stretch, y_stretch, joined_layout)
    )
    return (grad_in, grad_w_one, grad_w_two, grad_w_trans)


def solution(mesh):
    return jax.shard_map(
        body,
        mesh=mesh,
        in_specs=(
            P(("grp", "gx"), "gy", None),
            P(("grp", "gx"), "gy", None),
            P(("grp", "gx"), "gy", None),
            P(),
            P(),
            P(),
            P(),
            P("grp", "gy", None, "gx"),
        ),
        out_specs=(
            P(("grp", "gx"), "gy", None),
            P("grp", None, None),
            P("grp", None, None),
            P("grp", None),
        ),
        check_vma=False,
    )
```

profile of v0, /device:TPU:0, one launch (start us, length us, event | category | flops | bytes accessed | tf_op | source)
XLA Modules:
  0.0 242.6 jit_solution(7582713262238297557)
XLA Ops:
  7.2 6.3 %all-to-all-start = ((bf16[8,4,8,128]{3,2,1,0:T(8,128)(2,1)}), bf16[8,4,8,128]{3,2,1,0:T(8,128)(2,1)S(1)}, u32[]{:S(2)}, u32[]{:S(2)}) async-start(bf16[8,4,8,128]{3,2,1,0:T(8,128)(2,1)} %param.15), calls=%async_computation | async-start | bytes 131072 | tf_op jit(solution)/shard_map/all_to_all | solution.py:124
  13.5 1.1 fusion.242
  23.4 1.3 collective-permute-start.1
  24.8 4.6 %collective-permute-start = (bf16[2,8,1024]{2,1,0:T(8,128)(2,1)S(1)}, bf16[2,8,1024]{2,1,0:T(8,128)(2,1)S(1)}, u32[]{:S(2)}, u32[]{:S(2)}) collective-permute-start(bf16[2,8,1024]{2,1,0:T(8,128)(2,1)S(1)} %slice.631), channel_id=1, source_target_pairs={{0,4},{4,8},{8,12},{1,5},{5,9},{9,13},{2,6},{6,10},{10,14},{3,7},{... | collective-permute-start | bytes 98312 | tf_op jit(solution)/shard_map/ppermute | solution.py:18
  29.8 1.3 fusion
  31.3 1.3 collective-permute-start.3
  32.6 3.0 %collective-permute-start.2 = (bf16[8,2,1024]{2,1,0:T(2,128)(2,1)S(1)}, bf16[8,2,1024]{2,1,0:T(2,128)(2,1)S(1)}, u32[]{:S(2)}, u32[]{:S(2)}) collective-permute-start(bf16[8,2,1024]{2,1,0:T(2,128)(2,1)S(1)} %get-tuple-element.147), channel_id=1, source_target_pairs={{0,1},{1,2},{2,3},{4,5},{5,6},{6,7},{8,9},{9,10},{10,11},{12,13},{... | collective-permute-start | bytes 98312 | tf_op jit(solution)/shard_map/ppermute | solution.py:18
  42.5 1.3 collective-permute-start.5
  44.0 4.6 %collective-permute-start.4 = (bf16[2,8,1024]{2,1,0:T(8,128)(2,1)S(1)}, bf16[2,8,1024]{2,1,0:T(8,128)(2,1)S(1)}, u32[]{:S(2)}, u32[]{:S(2)}) collective-permute-start(bf16[2,8,1024]{2,1,0:T(8,128)(2,1)S(1)} %slice.673), channel_id=1, source_target_pairs={{0,4},{4,8},{8,12},{1,5},{5,9},{9,13},{2,6},{6,10},{10,14},{3,7},{... | collective-permute-start | bytes 98312 | tf_op jit(solution)/shard_map/ppermute | solution.py:18
  50.1 1.3 collective-permute-start.7
  51.4 3.0 %collective-permute-start.6 = (bf16[8,2,1024]{2,1,0:T(2,128)(2,1)S(1)}, bf16[8,2,1024]{2,1,0:T(2,128)(2,1)S(1)}, u32[]{:S(2)}, u32[]{:S(2)}) collective-permute-start(bf16[8,2,1024]{2,1,0:T(2,128)(2,1)S(1)} %get-tuple-element.143), channel_id=1, source_target_pairs={{0,1},{1,2},{2,3},{4,5},{5,6},{6,7},{8,9},{9,10},{10,11},{12,13},{... | collective-permute-start | bytes 98312 | tf_op jit(solution)/shard_map/ppermute | solution.py:18
  54.5 1.3 collective-permute-start.9
  55.8 4.9 %collective-permute-start.8 = (bf16[2,8,2048]{2,1,0:T(8,128)(2,1)S(1)}, bf16[2,8,2048]{2,1,0:T(8,128)(2,1)S(1)}, u32[]{:S(2)}, u32[]{:S(2)}) collective-permute-start(bf16[2,8,2048]{2,1,0:T(8,128)(2,1)S(1)} %get-tuple-element.141), channel_id=1, source_target_pairs={{0,4},{4,8},{8,12},{1,5},{5,9},{9,13},{2,6},{6,10},{10,14},{3,7},{... | collective-permute-start | bytes 196616 | tf_op jit(solution)/shard_map/ppermute | solution.py:18
  62.7 1.3 collective-permute-start.11
  64.0 5.2 %collective-permute-start.10 = (bf16[8,2,2048]{2,1,0:T(2,128)(2,1)S(1)}, bf16[8,2,2048]{2,1,0:T(2,128)(2,1)S(1)}, u32[]{:S(2)}, u32[]{:S(2)}) collective-permute-start(bf16[8,2,2048]{2,1,0:T(2,128)(2,1)S(1)} %get-tuple-element.139), channel_id=1, source_target_pairs={{0,1},{1,2},{2,3},{4,5},{5,6},{6,7},{8,9},{9,10},{10,11},{12,13},{... | collective-permute-start | bytes 196616 | tf_op jit(solution)/shard_map/ppermute | solution.py:18
  73.8 1.6 pad_slice_fusion.19
  75.4 1.1 fusion.245
  76.8 1.6 pad_slice_fusion.1
  78.4 1.1 fusion.244
  104.6 1.2 copy.159
  124.3 1.2 copy.188
  131.5 99.4 %all-reduce.7.cloned.1.call-done = (f32[27,64,64]{2,1,0:T(8,128)}, f32[27,64,64]{2,1,0:T(8,128)}, f32[512,512]{1,0:T(8,128)}) async-done(((f32[27,64,64]{2,1,0:T(8,128)}, f32[27,64,64]{2,1,0:T(8,128)}, f32[512,512]{1,0:T(8,128)}), (f32[27,64,64]{2,1,0:T(8,128)}, f32[27,64,64]{2,1,0:T(8,128)}, f32[512,512]{1,0:T(8,128)})) %all-reduce.7.cloned.1.call-update) | async-done | bytes 1933328 | tf_op jit(solution)/shard_map/psum | solution.py:173
  230.9 2.3 copy.215
  234.7 1.0 copy.217
  (357 shorter events, 75.1 us)
Async XLA Ops:
  7.2 14.5 %all-to-all-start = ((bf16[8,4,8,128]{3,2,1,0:T(8,128)(2,1)}), bf16[8,4,8,128]{3,2,1,0:T(8,128)(2,1)S(1)}, u32[]{:S(2)}, u32[]{:S(2)}) async-start(bf16[8,4,8,128]{3,2,1,0:T(8,128)(2,1)} %param.15), calls=%async_computation | async-start | bytes 131072 | tf_op jit(solution)/shard_map/all_to_all | solution.py:124
  13.5 217.4 %all-reduce.7.cloned.1.call-start = ((), (), s32[]{:S(2)}) async-start(), calls=%async_computation.1 | async-start | bytes 5636096 | tf_op jit(solution)/shard_map/psum | solution.py:173
  13.5 1.2 copy-start.45
  14.7 1.0 copy-start.44
  23.4 7.8 %collective-permute-start.1 = (bf16[2,8,1024]{2,1,0:T(8,128)(2,1)S(1)}, bf16[2,8,1024]{2,1,0:T(8,128)(2,1)S(1)}, u32[]{:S(2)}, u32[]{:S(2)}) collective-permute-start(bf16[2,8,1024]{2,1,0:T(8,128)(2,1)S(1)} %slice.633), channel_id=1, source_target_pairs={{4,0},{8,4},{12,8},{5,1},{9,5},{13,9},{6,2},{10,6},{14,10},{7,3},{... | collective-permute-start | bytes 98312 | tf_op jit(solution)/shard_map/ppermute | solution.py:20
  24.8 6.4 %collective-permute-start = (bf16[2,8,1024]{2,1,0:T(8,128)(2,1)S(1)}, bf16[2,8,1024]{2,1,0:T(8,128)(2,1)S(1)}, u32[]{:S(2)}, u32[]{:S(2)}) collective-permute-start(bf16[2,8,1024]{2,1,0:T(8,128)(2,1)S(1)} %slice.631), channel_id=1, source_target_pairs={{0,4},{4,8},{8,12},{1,5},{5,9},{9,13},{2,6},{6,10},{10,14},{3,7},{... | collective-permute-start | bytes 98312 | tf_op jit(solution)/shard_map/ppermute | solution.py:18
  31.3 5.0 %collective-permute-start.3 = (bf16[8,2,1024]{2,1,0:T(2,128)(2,1)S(1)}, bf16[8,2,1024]{2,1,0:T(2,128)(2,1)S(1)}, u32[]{:S(2)}, u32[]{:S(2)}) collective-permute-start(bf16[8,2,1024]{2,1,0:T(2,128)(2,1)S(1)} %get-tuple-element.148), channel_id=1, source_target_pairs={{1,0},{2,1},{3,2},{5,4},{6,5},{7,6},{9,8},{10,9},{11,10},{13,12},{... | collective-permute-start | bytes 98312 | tf_op jit(solution)/shard_map/ppermute | solution.py:20
  32.6 3.9 %collective-permute-start.2 = (bf16[8,2,1024]{2,1,0:T(2,128)(2,1)S(1)}, bf16[8,2,1024]{2,1,0:T(2,128)(2,1)S(1)}, u32[]{:S(2)}, u32[]{:S(2)}) collective-permute-start(bf16[8,2,1024]{2,1,0:T(2,128)(2,1)S(1)} %get-tuple-element.147), channel_id=1, source_target_pairs={{0,1},{1,2},{2,3},{4,5},{5,6},{6,7},{8,9},{9,10},{10,11},{12,13},{... | collective-permute-start | bytes 98312 | tf_op jit(solution)/shard_map/ppermute | solution.py:18
  42.5 6.8 %collective-permute-start.5 = (bf16[2,8,1024]{2,1,0:T(8,128)(2,1)S(1)}, bf16[2,8,1024]{2,1,0:T(8,128)(2,1)S(1)}, u32[]{:S(2)}, u32[]{:S(2)}) collective-permute-start(bf16[2,8,1024]{2,1,0:T(8,128)(2,1)S(1)} %slice.675), channel_id=1, source_target_pairs={{4,0},{8,4},{12,8},{5,1},{9,5},{13,9},{6,2},{10,6},{14,10},{7,3},{... | collective-permute-start | bytes 98312 | tf_op jit(solution)/shard_map/ppermute | solution.py:20
  44.0 6.1 %collective-permute-start.4 = (bf16[2,8,1024]{2,1,0:T(8,128)(2,1)S(1)}, bf16[2,8,1024]{2,1,0:T(8,128)(2,1)S(1)}, u32[]{:S(2)}, u32[]{:S(2)}) collective-permute-start(bf16[2,8,1024]{2,1,0:T(8,128)(2,1)S(1)} %slice.673), channel_id=1, source_target_pairs={{0,4},{4,8},{8,12},{1,5},{5,9},{9,13},{2,6},{6,10},{10,14},{3,7},{... | collective-permute-start | bytes 98312 | tf_op jit(solution)/shard_map/ppermute | solution.py:18
  50.1 4.4 %copy-start.2 = (bf16[4,8,1024]{2,1,0:T(8,128)(2,1)S(1)}, bf16[4,8,1024]{2,1,0:T(8,128)(2,1)}, u32[]{:S(2)}) copy-start(bf16[4,8,1024]{2,1,0:T(8,128)(2,1)} %param.8) | copy-start | bytes 196612
  50.1 10.6 %collective-permute-start.7 = (bf16[8,2,1024]{2,1,0:T(2,128)(2,1)S(1)}, bf16[8,2,1024]{2,1,0:T(2,128)(2,1)S(1)}, u32[]{:S(2)}, u32[]{:S(2)}) collective-permute-start(bf16[8,2,1024]{2,1,0:T(2,128)(2,1)S(1)} %get-tuple-element.144), channel_id=1, source_target_pairs={{1,0},{2,1},{3,2},{5,4},{6,5},{7,6},{9,8},{10,9},{11,10},{13,12},{... | collective-permute-start | bytes 98312 | tf_op jit(solution)/shard_map/ppermute | solution.py:20
  51.4 9.3 %collective-permute-start.6 = (bf16[8,2,1024]{2,1,0:T(2,128)(2,1)S(1)}, bf16[8,2,1024]{2,1,0:T(2,128)(2,1)S(1)}, u32[]{:S(2)}, u32[]{:S(2)}) collective-permute-start(bf16[8,2,1024]{2,1,0:T(2,128)(2,1)S(1)} %get-tuple-element.143), channel_id=1, source_target_pairs={{0,1},{1,2},{2,3},{4,5},{5,6},{6,7},{8,9},{9,10},{10,11},{12,13},{... | collective-permute-start | bytes 98312 | tf_op jit(solution)/shard_map/ppermute | solution.py:18
  54.5 7.8 %collective-permute-start.9 = (bf16[2,8,2048]{2,1,0:T(8,128)(2,1)S(1)}, bf16[2,8,2048]{2,1,0:T(8,128)(2,1)S(1)}, u32[]{:S(2)}, u32[]{:S(2)}) collective-permute-start(bf16[2,8,2048]{2,1,0:T(8,128)(2,1)S(1)} %get-tuple-element.142), channel_id=1, source_target_pairs={{4,0},{8,4},{12,8},{5,1},{9,5},{13,9},{6,2},{10,6},{14,10},{7,3},{... | collective-permute-start | bytes 196616 | tf_op jit(solution)/shard_map/ppermute | solution.py:20
  55.8 6.8 %collective-permute-start.8 = (bf16[2,8,2048]{2,1,0:T(8,128)(2,1)S(1)}, bf16[2,8,2048]{2,1,0:T(8,128)(2,1)S(1)}, u32[]{:S(2)}, u32[]{:S(2)}) collective-permute-start(bf16[2,8,2048]{2,1,0:T(8,128)(2,1)S(1)} %get-tuple-element.141), channel_id=1, source_target_pairs={{0,4},{4,8},{8,12},{1,5},{5,9},{9,13},{2,6},{6,10},{10,14},{3,7},{... | collective-permute-start | bytes 196616 | tf_op jit(solution)/shard_map/ppermute | solution.py:18
  62.7 10.4 %collective-permute-start.11 = (bf16[8,2,2048]{2,1,0:T(2,128)(2,1)S(1)}, bf16[8,2,2048]{2,1,0:T(2,128)(2,1)S(1)}, u32[]{:S(2)}, u32[]{:S(2)}) collective-permute-start(bf16[8,2,2048]{2,1,0:T(2,128)(2,1)S(1)} %get-tuple-element.140), channel_id=1, source_target_pairs={{1,0},{2,1},{3,2},{5,4},{6,5},{7,6},{9,8},{10,9},{11,10},{13,12},{... | collective-permute-start | bytes 196616 | tf_op jit(solution)/shard_map/ppermute | solution.py:20
  64.0 9.1 %collective-permute-start.10 = (bf16[8,2,2048]{2,1,0:T(2,128)(2,1)S(1)}, bf16[8,2,2048]{2,1,0:T(2,128)(2,1)S(1)}, u32[]{:S(2)}, u32[]{:S(2)}) collective-permute-start(bf16[8,2,2048]{2,1,0:T(2,128)(2,1)S(1)} %get-tuple-element.139), channel_id=1, source_target_pairs={{0,1},{1,2},{2,3},{4,5},{5,6},{6,7},{8,9},{9,10},{10,11},{12,13},{... | collective-permute-start | bytes 196616 | tf_op jit(solution)/shard_map/ppermute | solution.py:18
  78.4 1.1 copy-start.38
  105.8 1.0 copy-start.18
  125.5 1.0 copy-start.49
  125.5 1.0 copy-start.57
  125.5 1.1 copy-start.59
  230.9 2.3 copy-start.1
  233.2 1.5 copy-start
  (50 other events, 44.5 us)
Sparse Core Ops, SparseCore 0:
  125.7 105.2 all-reduce.6
where the time goes:
time: 244 us; the launch traced here: 243 us
  waiting for transfers between devices  101 us (41%)
  local copies, waits for them, and re-layouts  72.1 us (30%)
  starting transfers between devices  39.3 us (16%)
  between operations  15.4 us (6%)
  matrix products  12.8 us (5%)
    psum x1, waiting for transfers between devices, body(): grad_w_one = lax.psum(one_term, ('gx', 'gy'))  99.4 us
    unnamed x124, local copies, waits for them, and re-layouts  47.6 us
    ppermute x6, starting transfers between devices, padded(): lax.ppermute(tail, axis, [(i, (i + 1) % count) for i in range(ends)])  25.3 us
    ppermute x6, starting transfers between devices, padded(): lax.ppermute(head, axis, [((i + 1) % count, i) for i in range(ends)])  7.75 us
    slice x58, local copies, waits for them, and re-layouts, weight_terms(): sliding_window[:, :, DILATION_STEP * tap_index:DILATION_STEP * tap_index...  6.75 us
    all_to_all x1, starting transfers between devices, body(): lax.all_to_all(out_grad, 'gx', split_axis=0, concat_axis=3, tiled=True)  6.33 us
    dot_general x18, matrix products, data_terms(): jnp.dot(columns, stacked[x_index * 3 + y_index], preferred_element_type=j...  6.06 us
    slice x20, local copies, waits for them, and re-layouts, data_terms(): stacked[x_index * 3 + y_index]  5.96 us
  transfers between devices with their start and end apart: 14, of which 4 were waited for; matrix products, arithmetic and copies ran while one was open for 7% of the time, Pallas kernels for 0%

commit v1 on v0

--- a/solution.py
+++ b/solution.py
@@ -3,6 +3,7 @@
 import jax.numpy as jnp
 from jax import lax
 from jax.sharding import PartitionSpec as P
+from jax.lax import psum
 
 DILATION_STEP = 2
 
@@ -170,7 +171,7 @@
     )
     grad_w_two = lax.psum(two_term, ("gx", "gy"))
     one_term = weight_terms(in_rim, first_backward) * factor
-    grad_w_one = lax.psum(one_term, ("gx", "gy"))
+    grad_w_one = psum(psum(one_term, "gy"), "gx")
     grad_in = (
         data_terms(one_grad_rim, w_one)
         .astype(jnp.bfloat16)

time: 244 us -> 307 us (1.26)
  waiting for transfers between devices: 101 us -> 167 us
  local copies, waits for them, and re-layouts: 72.1 us -> 69 us
    psum x1 -> x3, waiting for transfers between devices: 99.4 us -> 165 us  [the longest x1 101 us: body(): grad_w_two = lax.psum(two_term, ('gx', 'gy'))]
    unnamed x124 -> x118, local copies, waits for them, and re-layouts: 47.6 us -> 46.6 us
  transfers between devices with their start and end apart: 14 -> 16, of which waited for: 4 -> 6; matrix products, arithmetic and copies ran while one was open for 7% -> 7% of each run, Pallas kernels for 0% -> 0%
where the time goes in v1:
time: 307 us; the launch traced here: 305 us
  waiting for transfers between devices  167 us (54%)
  local copies, waits for them, and re-layouts  69 us (22%)
  starting transfers between devices  39.5 us (13%)
  between operations  15.2 us (5%)
  matrix products  12.8 us (4%)
    psum x1, waiting for transfers between devices, body(): grad_w_two = lax.psum(two_term, ('gx', 'gy'))  101 us
    psum x2, waiting for transfers between devices, body(): grad_w_one = psum(psum(one_term, 'gy'), 'gx')  64.8 us
    unnamed x118, local copies, waits for them, and re-layouts  46.6 us
    ppermute x6, starting transfers between devices, padded(): lax.ppermute(tail, axis, [(i, (i + 1) % count) for i in range(ends)])  25.3 us
    ppermute x6, starting transfers between devices, padded(): lax.ppermute(head, axis, [((i + 1) % count, i) for i in range(ends)])  7.75 us
    all_to_all x1, starting transfers between devices, body(): lax.all_to_all(out_grad, 'gx', split_axis=0, concat_axis=3, tiled=True)  6.33 us
  transfers between devices with their start and end apart: 16, of which 6 were waited for; matrix products, arithmetic and copies ran while one was open for 7% of the time, Pallas kernels for 0%

profile of v1, /device:TPU:0, one launch (start us, length us, event | category | flops | bytes accessed | tf_op | source)
XLA Modules:
  0.0 305.5 jit_solution(9193384686141841954)
XLA Ops:
  7.2 6.3 %all-to-all-start = ((bf16[8,4,8,128]{3,2,1,0:T(8,128)(2,1)}), bf16[8,4,8,128]{3,2,1,0:T(8,128)(2,1)S(1)}, u32[]{:S(2)}, u32[]{:S(2)}) async-start(bf16[8,4,8,128]{3,2,1,0:T(8,128)(2,1)} %param.15), calls=%async_computation | async-start | bytes 131072 | tf_op jit(solution)/shard_map/all_to_all | solution.py:125
  22.2 1.3 collective-permute-start.1
  23.6 4.6 %collective-permute-start = (bf16[2,8,1024]{2,1,0:T(8,128)(2,1)S(1)}, bf16[2,8,1024]{2,1,0:T(8,128)(2,1)S(1)}, u32[]{:S(2)}, u32[]{:S(2)}) collective-permute-start(bf16[2,8,1024]{2,1,0:T(8,128)(2,1)S(1)} %slice.631), channel_id=1, source_target_pairs={{0,4},{4,8},{8,12},{1,5},{5,9},{9,13},{2,6},{6,10},{10,14},{3,7},{... | collective-permute-start | bytes 98312 | tf_op jit(solution)/shard_map/ppermute | solution.py:19
  28.6 1.3 fusion
  30.1 1.3 collective-permute-start.3
  31.4 3.0 collective-permute-start.2
  41.5 1.3 collective-permute-start.5
  42.9 4.6 %collective-permute-start.4 = (bf16[2,8,1024]{2,1,0:T(8,128)(2,1)S(1)}, bf16[2,8,1024]{2,1,0:T(8,128)(2,1)S(1)}, u32[]{:S(2)}, u32[]{:S(2)}) collective-permute-start(bf16[2,8,1024]{2,1,0:T(8,128)(2,1)S(1)} %slice.673), channel_id=1, source_target_pairs={{0,4},{4,8},{8,12},{1,5},{5,9},{9,13},{2,6},{6,10},{10,14},{3,7},{... | collective-permute-start | bytes 98312 | tf_op jit(solution)/shard_map/ppermute | solution.py:19
  47.6 1.4 collective-permute-done.4
  49.1 1.3 collective-permute-start.7
  50.4 3.0 collective-permute-start.6
  53.5 1.3 collective-permute-start.9
  54.8 4.9 %collective-permute-start.8 = (bf16[2,8,2048]{2,1,0:T(8,128)(2,1)S(1)}, bf16[2,8,2048]{2,1,0:T(8,128)(2,1)S(1)}, u32[]{:S(2)}, u32[]{:S(2)}) collective-permute-start(bf16[2,8,2048]{2,1,0:T(8,128)(2,1)S(1)} %get-tuple-element.140), channel_id=1, source_target_pairs={{0,4},{4,8},{8,12},{1,5},{5,9},{9,13},{2,6},{6,10},{10,14},{3,7},{... | collective-permute-start | bytes 196616 | tf_op jit(solution)/shard_map/ppermute | solution.py:19
  61.6 1.3 collective-permute-start.11
  62.9 5.3 %collective-permute-start.10 = (bf16[8,2,2048]{2,1,0:T(2,128)(2,1)S(1)}, bf16[8,2,2048]{2,1,0:T(2,128)(2,1)S(1)}, u32[]{:S(2)}, u32[]{:S(2)}) collective-permute-start(bf16[8,2,2048]{2,1,0:T(2,128)(2,1)S(1)} %get-tuple-element.138), channel_id=1, source_target_pairs={{0,1},{1,2},{2,3},{4,5},{5,6},{6,7},{8,9},{9,10},{10,11},{12,13},{... | collective-permute-start | bytes 196616 | tf_op jit(solution)/shard_map/ppermute | solution.py:19
  73.1 1.6 pad_slice_fusion.19
  74.7 1.1 fusion.245
  76.2 1.5 pad_slice_fusion.1
  104.8 1.2 copy.159
  122.4 21.8 %all-reduce.9.cloned.1.call-done = f32[27,64,64]{2,1,0:T(8,128)} async-done(((f32[27,64,64]{2,1,0:T(8,128)}), f32[27,64,64]{2,1,0:T(8,128)}) %all-reduce.9.cloned.1.call-update) | async-done | bytes 442384 | tf_op jit(solution)/shard_map/psum | solution.py:174
  144.6 1.2 copy.188
  150.5 43.0 %all-reduce.11.cloned.1.call-done = f32[27,64,64]{2,1,0:T(8,128)} async-done(((f32[27,64,64]{2,1,0:T(8,128)}), f32[27,64,64]{2,1,0:T(8,128)}) %all-reduce.11.cloned.1.call-update) | async-done | bytes 442384 | tf_op jit(solution)/shard_map/psum | solution.py:174
  193.5 100.7 %all-reduce.13.cloned.1.call-done = (f32[27,64,64]{2,1,0:T(8,128)}, f32[512,512]{1,0:T(8,128)}) async-done(((f32[27,64,64]{2,1,0:T(8,128)}, f32[512,512]{1,0:T(8,128)}), (f32[27,64,64]{2,1,0:T(8,128)}, f32[512,512]{1,0:T(8,128)})) %all-reduce.13.cloned.1.call-update) | async-done | bytes 1490960 | tf_op jit(solution)/shard_map/psum | solution.py:172
  294.2 2.3 copy.216
  (357 shorter events, 73.8 us)
Async XLA Ops:
  7.2 13.4 %all-to-all-start = ((bf16[8,4,8,128]{3,2,1,0:T(8,128)(2,1)}), bf16[8,4,8,128]{3,2,1,0:T(8,128)(2,1)S(1)}, u32[]{:S(2)}, u32[]{:S(2)}) async-start(bf16[8,4,8,128]{3,2,1,0:T(8,128)(2,1)} %param.15), calls=%async_computation | async-start | bytes 131072 | tf_op jit(solution)/shard_map/all_to_all | solution.py:125
  13.5 130.7 %all-reduce.9.cloned.1.call-start = ((), (), s32[]{:S(2)}) async-start(), calls=%async_computation.1 | async-start | bytes 1769472 | tf_op jit(solution)/shard_map/psum | solution.py:174
  13.5 1.2 copy-start.45
  14.7 1.0 copy-start.44
  22.2 7.8 %collective-permute-start.1 = (bf16[2,8,1024]{2,1,0:T(8,128)(2,1)S(1)}, bf16[2,8,1024]{2,1,0:T(8,128)(2,1)S(1)}, u32[]{:S(2)}, u32[]{:S(2)}) collective-permute-start(bf16[2,8,1024]{2,1,0:T(8,128)(2,1)S(1)} %slice.633), channel_id=1, source_target_pairs={{4,0},{8,4},{12,8},{5,1},{9,5},{13,9},{6,2},{10,6},{14,10},{7,3},{... | collective-permute-start | bytes 98312 | tf_op jit(solution)/shard_map/ppermute | solution.py:21
  23.6 6.4 %collective-permute-start = (bf16[2,8,1024]{2,1,0:T(8,128)(2,1)S(1)}, bf16[2,8,1024]{2,1,0:T(8,128)(2,1)S(1)}, u32[]{:S(2)}, u32[]{:S(2)}) collective-permute-start(bf16[2,8,1024]{2,1,0:T(8,128)(2,1)S(1)} %slice.631), channel_id=1, source_target_pairs={{0,4},{4,8},{8,12},{1,5},{5,9},{9,13},{2,6},{6,10},{10,14},{3,7},{... | collective-permute-start | bytes 98312 | tf_op jit(solution)/shard_map/ppermute | solution.py:19
  30.1 5.0 %collective-permute-start.3 = (bf16[8,2,1024]{2,1,0:T(2,128)(2,1)S(1)}, bf16[8,2,1024]{2,1,0:T(2,128)(2,1)S(1)}, u32[]{:S(2)}, u32[]{:S(2)}) collective-permute-start(bf16[8,2,1024]{2,1,0:T(2,128)(2,1)S(1)} %get-tuple-element.147), channel_id=1, source_target_pairs={{1,0},{2,1},{3,2},{5,4},{6,5},{7,6},{9,8},{10,9},{11,10},{13,12},{... | collective-permute-start | bytes 98312 | tf_op jit(solution)/shard_map/ppermute | solution.py:21
  31.4 3.9 %collective-permute-start.2 = (bf16[8,2,1024]{2,1,0:T(2,128)(2,1)S(1)}, bf16[8,2,1024]{2,1,0:T(2,128)(2,1)S(1)}, u32[]{:S(2)}, u32[]{:S(2)}) collective-permute-start(bf16[8,2,1024]{2,1,0:T(2,128)(2,1)S(1)} %get-tuple-element.146), channel_id=1, source_target_pairs={{0,1},{1,2},{2,3},{4,5},{5,6},{6,7},{8,9},{9,10},{10,11},{12,13},{... | collective-permute-start | bytes 98312 | tf_op jit(solution)/shard_map/ppermute | solution.py:19
  41.5 6.1 %collective-permute-start.5 = (bf16[2,8,1024]{2,1,0:T(8,128)(2,1)S(1)}, bf16[2,8,1024]{2,1,0:T(8,128)(2,1)S(1)}, u32[]{:S(2)}, u32[]{:S(2)}) collective-permute-start(bf16[2,8,1024]{2,1,0:T(8,128)(2,1)S(1)} %slice.675), channel_id=1, source_target_pairs={{4,0},{8,4},{12,8},{5,1},{9,5},{13,9},{6,2},{10,6},{14,10},{7,3},{... | collective-permute-start | bytes 98312 | tf_op jit(solution)/shard_map/ppermute | solution.py:21
  42.9 6.1 %collective-permute-start.4 = (bf16[2,8,1024]{2,1,0:T(8,128)(2,1)S(1)}, bf16[2,8,1024]{2,1,0:T(8,128)(2,1)S(1)}, u32[]{:S(2)}, u32[]{:S(2)}) collective-permute-start(bf16[2,8,1024]{2,1,0:T(8,128)(2,1)S(1)} %slice.673), channel_id=1, source_target_pairs={{0,4},{4,8},{8,12},{1,5},{5,9},{9,13},{2,6},{6,10},{10,14},{3,7},{... | collective-permute-start | bytes 98312 | tf_op jit(solution)/shard_map/ppermute | solution.py:19
  49.0 4.4 %copy-start.2 = (bf16[4,8,1024]{2,1,0:T(8,128)(2,1)S(1)}, bf16[4,8,1024]{2,1,0:T(8,128)(2,1)}, u32[]{:S(2)}) copy-start(bf16[4,8,1024]{2,1,0:T(8,128)(2,1)} %param.8) | copy-start | bytes 196612
  49.1 10.6 %collective-permute-start.7 = (bf16[8,2,1024]{2,1,0:T(2,128)(2,1)S(1)}, bf16[8,2,1024]{2,1,0:T(2,128)(2,1)S(1)}, u32[]{:S(2)}, u32[]{:S(2)}) collective-permute-start(bf16[8,2,1024]{2,1,0:T(2,128)(2,1)S(1)} %get-tuple-element.143), channel_id=1, source_target_pairs={{1,0},{2,1},{3,2},{5,4},{6,5},{7,6},{9,8},{10,9},{11,10},{13,12},{... | collective-permute-start | bytes 98312 | tf_op jit(solution)/shard_map/ppermute | solution.py:21
  50.4 9.3 %collective-permute-start.6 = (bf16[8,2,1024]{2,1,0:T(2,128)(2,1)S(1)}, bf16[8,2,1024]{2,1,0:T(2,128)(2,1)S(1)}, u32[]{:S(2)}, u32[]{:S(2)}) collective-permute-start(bf16[8,2,1024]{2,1,0:T(2,128)(2,1)S(1)} %get-tuple-element.142), channel_id=1, source_target_pairs={{0,1},{1,2},{2,3},{4,5},{5,6},{6,7},{8,9},{9,10},{10,11},{12,13},{... | collective-permute-start | bytes 98312 | tf_op jit(solution)/shard_map/ppermute | solution.py:19
  53.5 7.8 %collective-permute-start.9 = (bf16[2,8,2048]{2,1,0:T(8,128)(2,1)S(1)}, bf16[2,8,2048]{2,1,0:T(8,128)(2,1)S(1)}, u32[]{:S(2)}, u32[]{:S(2)}) collective-permute-start(bf16[2,8,2048]{2,1,0:T(8,128)(2,1)S(1)} %get-tuple-element.141), channel_id=1, source_target_pairs={{4,0},{8,4},{12,8},{5,1},{9,5},{13,9},{6,2},{10,6},{14,10},{7,3},{... | collective-permute-start | bytes 196616 | tf_op jit(solution)/shard_map/ppermute | solution.py:21
  54.8 6.8 %collective-permute-start.8 = (bf16[2,8,2048]{2,1,0:T(8,128)(2,1)S(1)}, bf16[2,8,2048]{2,1,0:T(8,128)(2,1)S(1)}, u32[]{:S(2)}, u32[]{:S(2)}) collective-permute-start(bf16[2,8,2048]{2,1,0:T(8,128)(2,1)S(1)} %get-tuple-element.140), channel_id=1, source_target_pairs={{0,4},{4,8},{8,12},{1,5},{5,9},{9,13},{2,6},{6,10},{10,14},{3,7},{... | collective-permute-start | bytes 196616 | tf_op jit(solution)/shard_map/ppermute | solution.py:19
  61.6 10.7 %collective-permute-start.11 = (bf16[8,2,2048]{2,1,0:T(2,128)(2,1)S(1)}, bf16[8,2,2048]{2,1,0:T(2,128)(2,1)S(1)}, u32[]{:S(2)}, u32[]{:S(2)}) collective-permute-start(bf16[8,2,2048]{2,1,0:T(2,128)(2,1)S(1)} %get-tuple-element.139), channel_id=1, source_target_pairs={{1,0},{2,1},{3,2},{5,4},{6,5},{7,6},{9,8},{10,9},{11,10},{13,12},{... | collective-permute-start | bytes 196616 | tf_op jit(solution)/shard_map/ppermute | solution.py:21
  62.9 9.4 %collective-permute-start.10 = (bf16[8,2,2048]{2,1,0:T(2,128)(2,1)S(1)}, bf16[8,2,2048]{2,1,0:T(2,128)(2,1)S(1)}, u32[]{:S(2)}, u32[]{:S(2)}) collective-permute-start(bf16[8,2,2048]{2,1,0:T(2,128)(2,1)S(1)} %get-tuple-element.138), channel_id=1, source_target_pairs={{0,1},{1,2},{2,3},{4,5},{5,6},{6,7},{8,9},{9,10},{10,11},{12,13},{... | collective-permute-start | bytes 196616 | tf_op jit(solution)/shard_map/ppermute | solution.py:19
  77.7 1.1 copy-start.38
  106.1 87.4 %all-reduce.11.cloned.1.call-start = ((), (), s32[]{:S(2)}) async-start(), calls=%async_computation.2 | async-start | bytes 1769472 | tf_op jit(solution)/shard_map/psum | solution.py:174
  144.2 150.0 %all-reduce.13.cloned.1.call-start = ((), (), s32[]{:S(2)}) async-start(), calls=%async_computation.3 | async-start | bytes 3866624 | tf_op jit(solution)/shard_map/psum | solution.py:172
  145.8 1.0 copy-start.54
  145.8 1.1 copy-start.56
  294.2 2.3 copy-start.1
  296.4 1.5 copy-start
  (49 other events, 44.0 us)
Sparse Core Ops, SparseCore 0:
  106.2 37.9 all-reduce.8
  146.5 46.9 all-reduce.10
  197.7 96.4 all-reduce.12
